TPU v7x, 128 devices: a whole 4x4x4 slice. The times are simulated.
128 devices in a mesh: dp: 2 (over core), tensor: 64 (over x, z, y).
Axes of the slice: x: 4, y: 4, z: 4, core: 2. Of those that a mesh axis runs over, the one named last changes fastest.
Arguments:
- hidden: bfloat16 [2048, 4096], P(('dp', 'tensor')), parts along dimension 0
- norm_gain: float32 [4096], replicated, may hold values from 0.3 to 3
- head_weight: bfloat16 [256512, 4096], P(('dp', 'tensor')), parts along dimension 0
- targets: int32 [2048], P(('dp', 'tensor')), parts along dimension 0, may hold values from 0 to 128255
- lengths: int32 [24], P('dp'), parts along dimension 0, may hold values from 1 to 256, as said below
- offsets: int32 [24], P('dp'), parts along dimension 0, may hold values from 0 to 1023, as said below
- loss_mask: int32 [2048], P(('dp', 'tensor')), parts along dimension 0, may hold values from 0 to 1, as said below
Outputs:
- token_logprob: float32 [2048], P(('dp', 'tensor')), parts along dimension 0
- token_entropy: float32 [2048], P(('dp', 'tensor')), parts along dimension 0
- sequence_score: float32 [24], P('dp'), parts along dimension 0
There are 2 independent parts, one for each index of `dp`. A program takes and returns all parts, laid end to end along the dimension named above; an argument that names none is the same for every part. Nothing has to cross between parts.
Inputs may be any that keep to these rules, and one draw needn't show every extreme that they name: `lengths`: responses lie in order and do not intersection within the 1024 rows; one has length exactly 256. offsets[k] + lengths[k] <= offsets[k+1], and the last response ends within the pack. `loss_mask`: ones only inside responses; the 16 rows of one index of tensor hold at most 10 ones, exactly 10 on some index.
All inputs are finite; a program needn't handle non-finite values.
Results may differ from a plain program's by a relative error of at most 0.0065.
The roundings to bfloat16 on the way count: a program that leaves them out, or rounds other values in their place, can miss the bound.
Values may be sent and summed in bfloat16 or wider, within the bound.
No kernel may reach another device: no remote copies, remote signals or barrier semaphores. Data moves between devices by JAX's collectives and lax.ppermute only.
A program may use at most 128 MiB of HBM per device.

v0:
```python
import jax
import jax.numpy as jnp
from jax import lax
from jax.sharding import PartitionSpec as P

epsilon = 1e-05


def row_stats(gathered, gathered_ids, head_weight, vocab_start):
    peaks, sums, spreads, pickeds = ([], [], [], [])
    for row_begin in range(0, gathered.shape[0], 512):
        row_block = gathered[row_begin : row_begin + 512]
        block_ids = gathered_ids[row_begin : row_begin + 512]
        scores = lax.dot_general(
            head_weight, row_block, (((1,), (1,)), ((), ())), preferred_element_type=jnp.float32
        )
        row_peak = jnp.max(scores, axis=0)
        centred = scores - row_peak[None, :]
        expo = jnp.exp(centred)
        sums.append(jnp.sum(expo, axis=0))
        spreads.append(jnp.sum(expo * centred, axis=0))
        column = vocab_start + lax.broadcasted_iota(jnp.int32, scores.shape, 0)
        pickeds.append(jnp.sum(jnp.where(column == block_ids[None, :], scores, 0.0), axis=0))
        peaks.append(row_peak)
    return (
        jnp.concatenate(peaks),
        jnp.concatenate(sums),
        jnp.concatenate(spreads),
        jnp.concatenate(pickeds),
    )


def rescaled(row_peak, row_sum, row_spread, global_peak):
    shift_by = row_peak - global_peak
    factor = jnp.exp(shift_by)
    return (factor * row_sum, factor * (row_spread + shift_by * row_sum))


def local(hidden, norm_gain, head_weight, targets, lengths, offsets, loss_mask):
    own_rows = hidden.shape[0]
    values = hidden.astype(jnp.float32)
    meansq = jnp.mean(values * values, axis=1, keepdims=True)
    normed = (values * lax.rsqrt(meansq + epsilon) * norm_gain[None, :]).astype(jnp.bfloat16)
    width = normed.shape[0]
    gathered, gathered_ids = (
        lax.all_gather(normed, "tensor", axis=0, tiled=True),
        lax.all_gather(targets, "tensor", axis=0, tiled=True),
    )
    shard_index = lax.axis_index("tensor")
    vocab_start = shard_index * head_weight.shape[0]
    row_peak, row_sum, row_spread, picked = row_stats(
        gathered, gathered_ids, head_weight, vocab_start
    )
    own_start = shard_index * width
    global_peak = lax.pmax(row_peak, "tensor")
    scaled_sum, scaled_spread = rescaled(row_peak, row_sum, row_spread, global_peak)
    summed = lax.psum((scaled_sum, scaled_spread, picked), "tensor")
    sum_exp, spread, target_logit = [
        lax.dynamic_slice_in_dim(item, own_start, width) for item in summed
    ]
    final_peak = lax.dynamic_slice_in_dim(global_peak, own_start, width)
    log_total = jnp.log(sum_exp)
    logprob_rows = target_logit - final_peak - log_total
    entropy_rows = log_total - spread / sum_exp
    mask_float = loss_mask.astype(jnp.float32)
    token_logprob = logprob_rows * mask_float
    token_entropy = entropy_rows * mask_float
    positions = shard_index * own_rows + lax.broadcasted_iota(jnp.int32, (own_rows,), 0)
    inside = (positions[None, :] >= offsets[:, None]) & (
        positions[None, :] < (offsets + lengths)[:, None]
    )
    partial_sums = jnp.sum(jnp.where(inside, token_logprob[None, :], 0.0), axis=1)
    seq_totals = lax.psum(partial_sums, "tensor")
    sequence_score = seq_totals / lengths.astype(jnp.float32)
    return (token_logprob, token_entropy, sequence_score)


def solution(mesh):
    return jax.shard_map(
        local,
        mesh=mesh,
        in_specs=(
            P(("dp", "tensor"), None),
            P(),
            P(("dp", "tensor"), None),
            P(("dp", "tensor")),
            P("dp"),
            P("dp"),
            P(("dp", "tensor")),
        ),
        out_specs=(P(("dp", "tensor")), P(("dp", "tensor")), P("dp")),
        check_vma=False,
    )
```

profile of v0, /device:TPU:0, one launch (start us, length us, event | category | flops | bytes accessed | tf_op | source)
XLA Modules:
  0.0 659.3 jit_solution(6251111973607725108)
XLA Ops:
  7.2 0.0 all-gather.2.cloned.1.call-start
  7.2 1.1 fusion.8
  8.3 1.7 fusion.10
  9.9 0.0 all-gather.2.cloned.1.call-update
  10.0 1.2 dynamic-slice
  11.9 0.7 add.54
  12.5 0.8 dynamic-update-slice
  13.4 25.3 %all-reduce = s32[1024]{0:T(1024)S(1)} all-reduce(s32[1024]{0:T(1024)S(1)} %dynamic-update-slice), channel_id=1, replica_groups=mesh['dp'=2,'tensor'=64] {'tensor'}, use_global_device_ids=true, to_apply=%add | all-reduce | flops 1024 | bytes 8192
  38.7 53.0 %all-gather.2.cloned.1.call-done = bf16[1024,4096]{1,0:T(8,128)(2,1)} async-done(((bf16[16,4096]{1,0:T(8,128)(2,1)}), bf16[1024,4096]{1,0:T(8,128)(2,1)}) %all-gather.2.cloned.1.call-update) | async-done | bytes 8388624 | tf_op jit(solution)/shard_map/all_gather | solution.py:46
  91.8 0.0 copy-start.3
  91.8 15.3 %fusion.13 = (f32[512]{0:T(512)S(1)}, f32[512,2004]{0,1:T(8,128)}) fusion(bf16[2004,4096]{1,0:T(8,128)(2,1)} %param.9, bf16[1024,4096]{1,0:T(8,128)(2,1)} %all-gather.2.cloned.1.call-done), kind=kOutput, calls=%fused_computation.35 | convolution fusion | flops 8406410752 | bytes 24750080 | tf_op jit(solution)/shard_map/dot_general | solution.py:14
  107.1 0.0 copy-done.3
  107.1 12.4 %fusion.14 = (f32[512]{0:T(512)S(1)}, f32[512,2004]{0,1:T(8,128)}) fusion(bf16[2004,4096]{1,0:T(8,128)(2,1)S(1)} %copy-done.3, bf16[1024,4096]{1,0:T(8,128)(2,1)} %all-gather.2.cloned.1.call-done), kind=kOutput, calls=%fused_computation.36 | convolution fusion | flops 8406410752 | bytes 24717312 | tf_op jit(solution)/shard_map/dot_general | solution.py:14
  119.5 176.9 %pmax.7 = f32[1024]{0:T(1024)S(1)} all-reduce(f32[1024]{0:T(1024)S(1)} %pad_maximum_fusion.1), channel_id=1, replica_groups=mesh['dp'=2,'tensor'=64] {'tensor'}, use_global_device_ids=true, to_apply=%region_6.7 | all-reduce | flops 1024 | bytes 8192 | tf_op jit(solution)/shard_map/pmax | solution.py:55
  296.5 0.0 copy-start
  296.5 0.0 copy-start.2
  296.5 0.0 copy-start.4
  296.5 5.0 fusion.4
  301.5 173.8 %all-reduce.2 = (f32[1024]{0:T(1024)S(1)}, f32[1024]{0:T(1024)S(1)}) all-reduce(f32[1024]{0:T(1024)S(1)} %pad_maximum_fusion, f32[1024]{0:T(1024)S(1)} %get-tuple-element.14), channel_id=1, replica_groups=mesh['dp'=2,'tensor'=64] {'tensor'}, use_global_device_ids=true, to_apply=%region_3.0 | all-reduce | flops 2048 | bytes 16384 | tf_op jit(solution)/shard_map/psum | solution.py:57
  475.3 0.0 copy-done
  475.3 0.1 convert_multiply_fusion.2
  475.4 0.0 copy-done.2
  475.4 0.0 copy-start.1
  475.4 0.2 select_reduce_fusion
  475.6 175.7 %all-reduce.1 = (f32[1024]{0:T(1024)S(1)}, f32[12]{0:T(128)S(1)}) all-reduce(f32[1024]{0:T(1024)S(1)} %get-tuple-element.13, f32[12]{0:T(128)S(1)} %select_reduce_fusion), channel_id=1, replica_groups=mesh['dp'=2,'tensor'=64] {'tensor'}, use_global_device_ids=true, to_apply=%region_12.13 | all-reduce | flops 1036 | bytes 8288 | tf_op jit(solution)/shard_map/psum | solution.py:57
  651.3 0.0 copy-done.4
  651.3 0.5 convert_divide_fusion
  651.9 0.6 subtract_multiply_fusion
  652.5 0.0 copy-done.1
  (8 shorter events, 0.1 us)
Async XLA Ops:
  7.2 84.6 %all-gather.2.cloned.1.call-start = ((), (), s32[]{:S(2)}) async-start(), calls=%async_computation | async-start | bytes 8519680 | tf_op jit(solution)/shard_map/all_gather | solution.py:46
  91.8 15.3 %copy-start.3 = (bf16[2004,4096]{1,0:T(8,128)(2,1)S(1)}, bf16[2004,4096]{1,0:T(8,128)(2,1)}, u32[]{:S(2)}) copy-start(bf16[2004,4096]{1,0:T(8,128)(2,1)} %param.9) | copy-start | bytes 49250308
  296.5 178.9 %copy-start = (s32[16]{0:T(128)S(1)}, s32[16]{0:T(128)}, u32[]{:S(2)}) copy-start(s32[16]{0:T(128)} %param.13) | copy-start | bytes 196
  296.5 178.9 %copy-start.2 = (s32[12]{0:T(128)S(1)}, s32[12]{0:T(128)}, u32[]{:S(2)}) copy-start(s32[12]{0:T(128)} %param.12) | copy-start | bytes 148
  296.5 354.9 %copy-start.4 = (s32[12]{0:T(128)S(1)}, s32[12]{0:T(128)}, u32[]{:S(2)}) copy-start(s32[12]{0:T(128)} %param.11) | copy-start | bytes 148
  475.4 177.1 %copy-start.1 = (f32[16]{0:T(128)}, f32[16]{0:T(128)S(1)}, u32[]{:S(2)}) copy-start(f32[16]{0:T(128)S(1)} %convert_multiply_fusion.2) | copy-start | bytes 196
Sparse Core Ops, SparseCore 0:
  10.8 80.8 all-gather.1
where the time goes:
time: 660 us; the launch traced here: 659 us
  blocking collectives  552 us (84%)
  waiting for transfers between devices  53.1 us (8%)
  matrix products  27.8 us (4%)
  between operations  14.8 us (2%)
  other arithmetic  9.77 us (1%)
    psum x2, blocking collectives, local(): summed = lax.psum((scaled_sum, scaled_spread, picked), 'tensor')  350 us
    pmax x1, blocking collectives, local(): global_peak = lax.pmax(row_peak, 'tensor')  177 us
    all_gather x1, waiting for transfers between devices, local(): lax.all_gather(normed, 'tensor', axis=0, tiled=True)  53 us
    dot_general x2, matrix products, row_stats(): lax.dot_general(head_weight, row_block, (((1,), (1,)), ((), ())), preferr...  27.8 us
    unnamed x1, blocking collectives  25.3 us
  transfers between devices with their start and end apart: 1, of which 1 were waited for; matrix products, arithmetic and copies ran while one was open for 0% of the time, Pallas kernels for 0%

commit v1 on v0

--- a/solution.py
+++ b/solution.py
@@ -43,7 +43,9 @@
     normed = (values * lax.rsqrt(meansq + epsilon) * norm_gain[None, :]).astype(jnp.bfloat16)
     width = normed.shape[0]
     gathered, gathered_ids = (
-        lax.all_gather(normed, "tensor", axis=0, tiled=True),
+        jnp.concatenate(
+            lax.all_to_all(jnp.stack([normed] * lax.axis_size("tensor")), "tensor", 0, 0), axis=0
+        ),
         lax.all_gather(targets, "tensor", axis=0, tiled=True),
     )
     shard_index = lax.axis_index("tensor")

time: 660 us -> 720 us (1.091)
  blocking collectives: 552 us -> 661 us
  waiting for transfers between devices: 53.1 us -> 0.01 us
  between operations: 14.8 us -> 1.42 us
  starting transfers between devices: 0.04 us -> 11.9 us
    unnamed x1, blocking collectives: 25.3 us -> 137 us
    all_gather x1 -> x0, waiting for transfers between devices: 53 us -> none  [local(): lax.all_gather(normed, 'tensor', axis=0, tiled=True)]
    all_to_all x0 -> x1, starting transfers between devices: none -> 11.9 us  [local(): lax.all_to_all(jnp.stack([normed] * lax.axis_size('tensor')), 'tensor', 0...]
  transfers between devices with their start and end apart: 1 -> 1, of which waited for: 1 -> 0; matrix products, arithmetic and copies ran while one was open for 0% -> 0% of each run, Pallas kernels for 0% -> 0%
where the time goes in v1:
time: 720 us
  blocking collectives  661 us (92%)
  matrix products  27.4 us (4%)
  starting transfers between devices  11.9 us (2%)
  local copies, waits for them, and re-layouts  9.12 us (1%)
  other arithmetic  8.43 us (1%)
    psum x2, blocking collectives, local(): summed = lax.psum((scaled_sum, scaled_spread, picked), 'tensor')  350 us
    pmax x1, blocking collectives, local(): global_peak = lax.pmax(row_peak, 'tensor')  175 us
    unnamed x1, blocking collectives  137 us
    dot_general x2, matrix products, row_stats(): lax.dot_general(head_weight, row_block, (((1,), (1,)), ((), ())), preferr...  27.4 us
  transfers between devices with their start and end apart: 1, of which 0 were waited for; matrix products, arithmetic and copies ran while one was open for 0% of the time, Pallas kernels for 0%

profile of v1, /device:TPU:0, one launch (start us, length us, event | category | flops | bytes accessed | tf_op | source)
XLA Modules:
  0.0 719.6 jit_solution(7359999379734520144)
XLA Ops:
  0.6 1.1 fusion.4
  1.7 1.0 fusion.6
  2.7 4.3 stack.2
  7.0 0.0 copy-start.5
  7.0 0.0 copy-start.2
  7.0 0.0 copy-start.4
  7.0 0.0 copy-start.3
  7.0 11.9 %all-to-all-start = ((bf16[64,16,4096]{2,1,0:T(8,128)(2,1)}), bf16[64,16,4096]{2,1,0:T(8,128)(2,1)}, u32[]{:S(2)}, u32[]{:S(2)}) async-start(bf16[64,16,4096]{2,1,0:T(8,128)(2,1)} %stack.2), calls=%async_computation | async-start | bytes 16777216 | tf_op jit(solution)/shard_map/all_to_all | solution.py:47
  18.9 0.0 copy-done.5
  18.9 0.6 dynamic-slice
  20.2 0.0 copy-done.2
  20.2 0.0 copy-done.4
  20.2 0.0 copy-done.3
  20.2 0.2 dynamic-update-slice
  20.5 137.0 %all-reduce = s32[1024]{0:T(1024)S(1)} all-reduce(s32[1024]{0:T(1024)S(1)} %dynamic-update-slice), channel_id=1, replica_groups=mesh['dp'=2,'tensor'=64] {'tensor'}, use_global_device_ids=true, to_apply=%add | all-reduce | flops 1024 | bytes 8192
  157.5 0.0 all-to-all-done
  157.5 4.0 fusion.8
  161.5 13.7 %fusion.10 = (f32[512]{0:T(512)S(1)}, f32[512,2004]{0,1:T(8,128)}) fusion(bf16[512,4096]{1,0:T(8,128)(2,1)S(1)} %bitcast.26, bf16[2004,4096]{1,0:T(8,128)(2,1)} %param.9), kind=kOutput, calls=%fused_computation.32 | convolution fusion | flops 8406410752 | bytes 24717312 | tf_op jit(solution)/shard_map/dot_general | solution.py:14
  175.2 13.7 %fusion.11 = (f32[512]{0:T(512)S(1)}, f32[512,2004]{0,1:T(8,128)}) fusion(bf16[512,4096]{1,0:T(8,128)(2,1)S(1)} %bitcast.25, bf16[2004,4096]{1,0:T(8,128)(2,1)} %param.9), kind=kOutput, calls=%fused_computation.33 | convolution fusion | flops 8406410752 | bytes 24717312 | tf_op jit(solution)/shard_map/dot_general | solution.py:14
  188.9 0.0 copy-start
  188.9 174.7 %pmax.7 = f32[1024]{0:T(1024)S(1)} all-reduce(f32[1024]{0:T(1024)S(1)} %pad_maximum_fusion.1), channel_id=1, replica_groups=mesh['dp'=2,'tensor'=64] {'tensor'}, use_global_device_ids=true, to_apply=%region_6.7 | all-reduce | flops 1024 | bytes 8192 | tf_op jit(solution)/shard_map/pmax | solution.py:57
  363.6 4.9 fusion
  368.6 173.9 %all-reduce.2 = (f32[1024]{0:T(1024)S(1)}, f32[1024]{0:T(1024)S(1)}) all-reduce(f32[1024]{0:T(1024)S(1)} %pad_maximum_fusion, f32[1024]{0:T(1024)S(1)} %get-tuple-element.16), channel_id=1, replica_groups=mesh['dp'=2,'tensor'=64] {'tensor'}, use_global_device_ids=true, to_apply=%region_3.0 | all-reduce | flops 2048 | bytes 16384 | tf_op jit(solution)/shard_map/psum | solution.py:59
  542.5 0.0 copy-done
  542.5 0.1 convert_multiply_fusion.2
  542.6 0.0 copy-start.1
  542.6 0.2 select_reduce_fusion
  542.7 175.7 %all-reduce.1 = (f32[1024]{0:T(1024)S(1)}, f32[12]{0:T(128)S(1)}) all-reduce(f32[1024]{0:T(1024)S(1)} %get-tuple-element.15, f32[12]{0:T(128)S(1)} %select_reduce_fusion), channel_id=1, replica_groups=mesh['dp'=2,'tensor'=64] {'tensor'}, use_global_device_ids=true, to_apply=%region_12.13 | all-reduce | flops 1036 | bytes 8288 | tf_op jit(solution)/shard_map/psum | solution.py:59
  718.5 0.5 convert_divide_fusion
  719.0 0.6 subtract_multiply_fusion
  719.6 0.0 copy-done.1
  (9 shorter events, 0.1 us)
Async XLA Ops:
  7.0 12.0 %copy-start.5 = (u32[128]{0:T(128)S(1)}, u32[128]{0:T(128)}, u32[]{:S(2)}) copy-start(u32[128]{0:T(128)} %constant.27) | copy-start | bytes 1540
  7.0 13.2 %copy-start.2 = (s32[12]{0:T(128)S(1)}, s32[12]{0:T(128)}, u32[]{:S(2)}) copy-start(s32[12]{0:T(128)} %param.12) | copy-start | bytes 148
  7.0 13.2 %copy-start.4 = (s32[12]{0:T(128)S(1)}, s32[12]{0:T(128)}, u32[]{:S(2)}) copy-start(s32[12]{0:T(128)} %param.11) | copy-start | bytes 148
  7.0 13.2 %copy-start.3 = (s32[16]{0:T(128)S(1)}, s32[16]{0:T(128)}, u32[]{:S(2)}) copy-start(s32[16]{0:T(128)} %param.10) | copy-start | bytes 196
  7.0 150.5 %all-to-all-start = ((bf16[64,16,4096]{2,1,0:T(8,128)(2,1)}), bf16[64,16,4096]{2,1,0:T(8,128)(2,1)}, u32[]{:S(2)}, u32[]{:S(2)}) async-start(bf16[64,16,4096]{2,1,0:T(8,128)(2,1)} %stack.2), calls=%async_computation | async-start | bytes 16777216 | tf_op jit(solution)/shard_map/all_to_all | solution.py:47
  188.9 353.6 %copy-start = (s32[16]{0:T(128)S(1)}, s32[16]{0:T(128)}, u32[]{:S(2)}) copy-start(s32[16]{0:T(128)} %param.13) | copy-start | bytes 196
  542.6 177.1 %copy-start.1 = (f32[16]{0:T(128)}, f32[16]{0:T(128)S(1)}, u32[]{:S(2)}) copy-start(f32[16]{0:T(128)S(1)} %convert_multiply_fusion.2) | copy-start | bytes 196
